TPU v7x, 32 devices: a whole 2x2x4 slice. The times are simulated.
32 devices in a mesh: groups: 2 (over x), mp: 16 (over z, y, core).
Axes of the slice: x: 2, y: 2, z: 4, core: 2. Of those that a mesh axis runs over, the one named last changes fastest.
Arguments:
- activations: bfloat16 [128, 16384], P(('groups', 'mp')), parts along dimension 0, may hold values from -6 to 6
- gain: bfloat16 [16384], replicated, may hold values from 0.5 to 1.5
- q_weight: bfloat16 [16384, 16384], P(None, 'mp'), may hold values from -0.046875 to 0.046875
- kv_weight: bfloat16 [16384, 2048], P(None, 'mp'), may hold values from -0.046875 to 0.046875
- o_weight: bfloat16 [16384, 16384], P(None, 'mp'), may hold values from -0.75 to 0.75
- key_cache: bfloat16 [128, 8, 512, 128], P(('groups', 'mp')), parts along dimension 0, may hold values from -400 to 400
- value_cache: bfloat16 [128, 8, 512, 128], P(('groups', 'mp')), parts along dimension 0, may hold values from -6 to 6
- lengths: int32 [128], P(('groups', 'mp')), parts along dimension 0, may hold values from 1 to 512, as said below
Outputs:
- attention_out: bfloat16 [128, 16384], P('groups', 'mp'), parts along dimension 0
There are 2 independent parts, one for each index of `groups`. A program takes and returns all parts, laid end to end along the dimension named above; an argument that names none is the same for every part. Nothing has to cross between parts.
Inputs may be any that keep to these rules, and one draw needn't show every extreme that they name: Request b attends to key_cache[b, :, t] and value_cache[b, :, t] for t < lengths[b]; some request has exactly 512.
All inputs are finite; a program needn't handle non-finite values.
Results may differ from a plain program's by a relative error of at most 0.007.
The roundings to bfloat16 on the way count: a program that leaves them out, or rounds other values in their place, can miss the bound.
Values may be sent and summed in bfloat16 or wider, within the bound.
A program may use at most 128 MiB of HBM per device.

v0:
```python
import math

import jax
import jax.numpy as jnp
from jax import lax
from jax.sharding import PartitionSpec as P

HEADS = 128
KV_HEADS = 8
HEAD_DIM = 128
CACHE = 512


rope_base = 500000.0
norm_eps = 1e-05


def rotate(vector, position):
    middle = vector.shape[-1] // 2
    offsets = jnp.arange(middle, dtype=jnp.float32)
    frequency = jnp.exp(offsets * (-2.0 * math.log(rope_base) / vector.shape[-1]))
    angles = position * frequency
    cosine = jnp.cos(angles)
    sine = jnp.sin(angles)
    leading = vector[..., :middle]
    trailing = vector[..., middle:]
    return jnp.concatenate(
        [leading * cosine - trailing * sine, trailing * cosine + leading * sine], axis=-1
    )


def normalize(activations, gain):
    widened = activations.astype(jnp.float32)
    inverse = lax.rsqrt(jnp.mean(widened * widened, axis=-1, keepdims=True) + norm_eps)
    return (widened * inverse * gain.astype(jnp.float32)).astype(jnp.bfloat16)


def shards(activations, gain, q_weight, kv_weight, o_weight, key_cache, value_cache, lengths):
    normed = normalize(activations, gain)
    piece = lax.all_gather(normed, "mp", axis=0, tiled=True)
    projected = jnp.concatenate(
        [
            jnp.dot(piece, q_weight, preferred_element_type=jnp.float32),
            jnp.dot(piece, kv_weight, preferred_element_type=jnp.float32),
        ],
        axis=1,
    ).astype(jnp.bfloat16)
    query_cols = q_weight.shape[1]
    query_all, pairs_all = (
        lax.all_to_all(projected[:, :query_cols], "mp", split_axis=0, concat_axis=1, tiled=True),
        lax.all_to_all(projected[:, query_cols:], "mp", split_axis=0, concat_axis=1, tiled=True),
    )
    requests = query_all.shape[0]
    per_group = HEADS // KV_HEADS
    scaling = 1.0 / math.sqrt(HEAD_DIM)
    position = lengths.astype(jnp.float32)
    query = rotate(
        query_all.astype(jnp.float32).reshape(requests, KV_HEADS, per_group, HEAD_DIM),
        position[:, None, None, None],
    ).astype(jnp.bfloat16)
    fresh_key = rotate(
        pairs_all[:, : KV_HEADS * HEAD_DIM]
        .astype(jnp.float32)
        .reshape(requests, KV_HEADS, HEAD_DIM),
        position[:, None, None],
    ).astype(jnp.bfloat16)
    fresh_value = pairs_all[:, KV_HEADS * HEAD_DIM :].reshape(requests, KV_HEADS, HEAD_DIM)
    scores = (
        jnp.einsum("rgqd,rgtd->rgqt", query, key_cache, preferred_element_type=jnp.float32)
        * scaling
    )
    visible = jnp.arange(CACHE, dtype=jnp.int32)[None, :] < lengths[:, None]
    scores = jnp.where(visible[:, None, None, :], scores, -1e30)
    own = (
        jnp.einsum("rgqd,rgd->rgq", query, fresh_key, preferred_element_type=jnp.float32) * scaling
    )
    highest = jnp.maximum(jnp.max(scores, axis=-1), own)
    weights = jnp.where(visible[:, None, None, :], jnp.exp(scores - highest[..., None]), 0.0)
    own_weight = jnp.exp(own - highest)
    denominator = jnp.sum(weights, axis=-1) + own_weight
    probs = (weights / denominator[..., None]).astype(jnp.bfloat16)
    own_prob = (own_weight / denominator).astype(jnp.bfloat16)
    mixed = jnp.einsum("rgqt,rgtd->rgqd", probs, value_cache, preferred_element_type=jnp.float32)
    mixed = (
        mixed
        + own_prob.astype(jnp.float32)[..., None] * fresh_value.astype(jnp.float32)[:, :, None, :]
    )
    attended = mixed.reshape(requests, HEADS * HEAD_DIM).astype(jnp.bfloat16)
    result = jnp.dot(
        lax.all_gather(attended, "mp", axis=0, tiled=True),
        o_weight,
        preferred_element_type=jnp.float32,
    )
    return result.astype(jnp.bfloat16)


def solution(mesh):
    placed = (
        P(("groups", "mp"), None),
        P(),
        P(None, "mp"),
        P(None, "mp"),
        P(None, "mp"),
        P(("groups", "mp"), None, None, None),
        P(("groups", "mp"), None, None, None),
        P(("groups", "mp")),
    )
    return jax.shard_map(
        shards, mesh=mesh, in_specs=placed, out_specs=P("groups", "mp"), check_vma=False
    )
```

profile of v0, /device:TPU:0, one launch (start us, length us, event | category | flops | bytes accessed | tf_op | source)
XLA Modules:
  0.0 161.7 jit_solution(6633450354537254687)
XLA Ops:
  6.5 0.0 all-gather.5.cloned.1.call-start
  6.5 0.8 convert_element_type.55
  7.3 1.2 fusion.7
  8.5 1.7 %fusion.10 = bf16[1,4,16384]{2,1,0:T(4,128)(2,1)} fusion(bf16[4,16384]{1,0:T(4,128)(2,1)} %param.8, f32[16384]{0:T(1024)S(1)} %convert_element_type.55, f32[4]{0:T(128)S(1)} %add_rsqrt_fusion), kind=kLoop, calls=%fused_computation.22 | loop fusion | flops 262144 | bytes 327696
  10.2 0.0 all-gather.5.cloned.1.call-update
  10.2 0.7 convert_element_type.60
  10.9 0.7 iota_compare_fusion
  11.6 0.1 multiply_cosine_fusion
  11.7 42.8 %all-gather.5.cloned.1.call-done = bf16[16,4,16384]{2,1,0:T(4,128)(2,1)} async-done(((bf16[1,4,16384]{2,1,0:T(4,128)(2,1)}), bf16[16,4,16384]{2,1,0:T(4,128)(2,1)}) %all-gather.5.cloned.1.call-update) | async-done | bytes 2097168 | tf_op jit(solution)/shard_map/all_gather | solution.py:40
  54.5 2.5 %reshape.180 = bf16[64,16384]{1,0:T(8,128)(2,1)S(1)} reshape(bf16[16,4,16384]{2,1,0:T(4,128)(2,1)} %all-gather.5.cloned.1.call-done) | data formatting | bytes 4194304
  57.1 3.6 %convolution_convert_fusion.2 = bf16[64,128]{1,0:T(8,128)(2,1)} fusion(bf16[64,16384]{1,0:T(8,128)(2,1)S(1)} %reshape.180, bf16[16384,128]{1,0:T(8,128)(2,1)} %param.11), kind=kOutput, calls=%fused_computation.6 | convolution fusion | flops 268443648 | bytes 6307840 | tf_op jit(solution)/shard_map/dot_general | solution.py:44
  60.7 3.5 %all-to-all-start.1 = ((bf16[16,4,128]{2,1,0:T(4,128)(2,1)}), bf16[16,4,128]{2,1,0:T(4,128)(2,1)S(1)}, u32[]{:S(2)}, u32[]{:S(2)}) async-start(bf16[16,4,128]{2,1,0:T(4,128)(2,1)} %bitcast.2), calls=%async_computation.1 | async-start | bytes 32768 | tf_op jit(solution)/shard_map/all_to_all | solution.py:51
  64.2 13.6 %convolution_convert_fusion.1 = bf16[64,1024]{1,0:T(8,128)(2,1)S(1)} fusion(bf16[64,16384]{1,0:T(8,128)(2,1)S(1)} %reshape.180, bf16[16384,1024]{1,0:T(8,128)(2,1)} %param.10), kind=kOutput, calls=%fused_computation.5 | convolution fusion | flops 2147549184 | bytes 35782656 | tf_op jit(solution)/shard_map/dot_general | solution.py:43
  77.8 0.7 all_to_all.24
  78.5 0.0 all-to-all-done.1
  78.5 6.0 %all-to-all-start = ((bf16[16,4,1024]{2,1,0:T(4,128)(2,1)}), bf16[16,4,1024]{2,1,0:T(4,128)(2,1)S(1)}, u32[]{:S(2)}, u32[]{:S(2)}) async-start(bf16[16,4,1024]{2,1,0:T(4,128)(2,1)} %all_to_all.24), calls=%async_computation | async-start | bytes 262144 | tf_op jit(solution)/shard_map/all_to_all | solution.py:50
  84.5 0.0 all-gather.7.cloned.1.call-start
  84.6 0.1 subtract_convert_fusion.1
  84.6 0.1 maximum_bitcast_fusion
  84.7 7.7 %all-to-all-done = bf16[16,4,1024]{2,1,0:T(4,128)(2,1)S(1)} async-done(((bf16[16,4,1024]{2,1,0:T(4,128)(2,1)}), bf16[16,4,1024]{2,1,0:T(4,128)(2,1)S(1)}, u32[]{:S(2)}, u32[]{:S(2)}) %all-to-all-start) | async-done | bytes 131104 | tf_op jit(solution)/shard_map/all_to_all | solution.py:50
  92.4 0.2 copy.10
  92.6 0.0 copy-start
  92.6 0.1 subtract_convert_fusion
  92.8 0.2 fusion.11
  93.0 3.7 %fusion.18 = (f32[4,8,16]{2,1,0:T(8,128)S(1)}, f32[4,8,16,512]{3,2,1,0:T(8,128)S(1)}) fusion(bf16[4,8,512,128]{3,2,1,0:T(8,128)(2,1)} %param.13, bf16[4,8,16,64]{3,2,1,0:T(8,128)(2,1)S(1)} %get-tuple-element.6, bf16[4,8,16,64]{3,2,1,0:T(8,128)(2,1)S(1)} %get-tuple-element.5, pred[4,512]{1,0:T(4,128)(4,1)S(1)} %iota_compare_fusion), kind=kOutput, calls=%fused_computation.46 | convolution fusion | flops 68156928 | bytes 5378048 | tf_op jit(solution)/shard_map/rgqd,rgtd->rgqt/dot_general | solution.py:69
  96.8 0.4 fusion.2
  97.2 0.0 copy-done
  97.2 0.8 fusion.1
  98.0 0.7 reshape.181
  98.7 0.0 all-gather.7.cloned.1.call-update
  98.7 39.4 %all-gather.7.cloned.1.call-done = bf16[16,4,16384]{2,1,0:T(4,128)(2,1)} async-done(((bf16[1,4,16384]{2,1,0:T(4,128)(2,1)}), bf16[16,4,16384]{2,1,0:T(4,128)(2,1)}) %all-gather.7.cloned.1.call-update) | async-done | bytes 2097168 | tf_op jit(solution)/shard_map/all_gather | solution.py:90
  138.1 2.5 %reshape.182 = bf16[64,16384]{1,0:T(8,128)(2,1)S(1)} reshape(bf16[16,4,16384]{2,1,0:T(4,128)(2,1)} %all-gather.7.cloned.1.call-done) | data formatting | bytes 4194304
  140.6 14.2 %convolution_convert_fusion = bf16[64,1024]{1,0:T(8,128)(2,1)} fusion(bf16[64,16384]{1,0:T(8,128)(2,1)S(1)} %reshape.182, bf16[16384,1024]{1,0:T(8,128)(2,1)} %param.12), kind=kOutput, calls=%fused_computation.4 | convolution fusion | flops 2147549184 | bytes 35782656 | tf_op jit(solution)/shard_map/dot_general | solution.py:89
  (8 shorter events, 0.1 us)
Async XLA Ops:
  6.5 48.0 %all-gather.5.cloned.1.call-start = ((), (), s32[]{:S(2)}) async-start(), calls=%async_computation.2 | async-start | bytes 2228224 | tf_op jit(solution)/shard_map/all_gather | solution.py:40
  60.7 17.8 %all-to-all-start.1 = ((bf16[16,4,128]{2,1,0:T(4,128)(2,1)}), bf16[16,4,128]{2,1,0:T(4,128)(2,1)S(1)}, u32[]{:S(2)}, u32[]{:S(2)}) async-start(bf16[16,4,128]{2,1,0:T(4,128)(2,1)} %bitcast.2), calls=%async_computation.1 | async-start | bytes 32768 | tf_op jit(solution)/shard_map/all_to_all | solution.py:51
  78.5 13.9 %all-to-all-start = ((bf16[16,4,1024]{2,1,0:T(4,128)(2,1)}), bf16[16,4,1024]{2,1,0:T(4,128)(2,1)S(1)}, u32[]{:S(2)}, u32[]{:S(2)}) async-start(bf16[16,4,1024]{2,1,0:T(4,128)(2,1)} %all_to_all.24), calls=%async_computation | async-start | bytes 262144 | tf_op jit(solution)/shard_map/all_to_all | solution.py:50
  84.5 53.6 %all-gather.7.cloned.1.call-start = ((), (), s32[]{:S(2)}) async-start(), calls=%async_computation.3 | async-start | bytes 2228224 | tf_op jit(solution)/shard_map/all_gather | solution.py:90
  92.6 4.5 %copy-start = (bf16[4,8,512,128]{3,2,1,0:T(8,128)(2,1)S(1)}, bf16[4,8,512,128]{3,2,1,0:T(8,128)(2,1)}, u32[]{:S(2)}) copy-start(bf16[4,8,512,128]{3,2,1,0:T(8,128)(2,1)} %param.14) | copy-start | bytes 12582916
Sparse Core Ops, SparseCore 0:
  10.3 44.1 all-gather.4
  98.8 39.1 all-gather.6
where the time goes:
time: 162 us
  waiting for transfers between devices  89.9 us (55%)
  matrix products  36.2 us (22%)
  between operations  13.5 us (8%)
  starting transfers between devices  9.48 us (6%)
  local copies, waits for them, and re-layouts  6.73 us (4%)
  other arithmetic  5.85 us (4%)
    all_gather x1, waiting for transfers between devices, shards(): piece = lax.all_gather(normed, 'mp', axis=0, tiled=True)  42.8 us
    all_gather x1, waiting for transfers between devices, shards(): lax.all_gather(attended, 'mp', axis=0, tiled=True)  39.4 us
    dot_general x1, matrix products, shards(): jnp.dot(lax.all_gather(attended, 'mp', axis=0, tiled=True), o_weight, pre...  14.2 us
    dot_general x1, matrix products, shards(): jnp.dot(piece, q_weight, preferred_element_type=jnp.float32)  13.6 us
    all_to_all x1, waiting for transfers between devices, shards(): lax.all_to_all(projected[:, :query_cols], 'mp', split_axis=0, concat_axis...  7.67 us
    all_to_all x1, starting transfers between devices, shards(): lax.all_to_all(projected[:, :query_cols], 'mp', split_axis=0, concat_axis...  5.97 us
    unnamed x5, local copies, waits for them, and re-layouts  5.81 us
    dot_general x1, matrix products, shards(): jnp.einsum('rgqd,rgtd->rgqt', query, key_cache, preferred_element_type=jn...  3.73 us
  transfers between devices with their start and end apart: 4, of which 3 were waited for; matrix products, arithmetic and copies ran while one was open for 9% of the time, Pallas kernels for 0%

commit v1 on v0

--- a/solution.py
+++ b/solution.py
@@ -1,14 +1,18 @@
+import functools
 import math
 
 import jax
 import jax.numpy as jnp
 from jax import lax
+from jax.experimental import pallas as pl
+from jax.experimental.pallas import tpu as pltpu
 from jax.sharding import PartitionSpec as P
 
 HEADS = 128
 KV_HEADS = 8
 HEAD_DIM = 128
 CACHE = 512
+MESH = pl.DeviceIdType.MESH
 
 
 rope_base = 500000.0
@@ -93,6 +97,417 @@
     )
     return result.astype(jnp.bfloat16)
 
+def layout_of(mesh):
+    row = mesh.devices.reshape(-1, mesh.shape["mp"])[0]
+    chips = [tuple(d.coords) for d in row]
+    cores = 1
+    while cores < len(chips) and chips[cores] == chips[0]:
+        cores += 1
+    chips = chips[::cores]
+    across = 1
+    if len(chips) > 1:
+        moved = [i for i in range(len(chips[0])) if chips[1][i] != chips[0][i]]
+        fixed = [i for i in range(len(chips[0])) if i not in moved]
+        while across < len(chips) and all(chips[across][i] == chips[0][i] for i in fixed):
+            across += 1
+    if len(chips) % across:
+        across = 1
+    return len(chips) // across, across, cores
+
+
+def fused(
+    dims,
+    act_ref,
+    gain_ref,
+    cos_ref,
+    sin_ref,
+    len_ref,
+    wq_ref,
+    wkv_ref,
+    wo_ref,
+    kc_ref,
+    vc_ref,
+    out_ref,
+    wbuf,
+    kvbuf,
+    kbuf,
+    vbuf,
+    x1,
+    x2,
+    acc,
+    acc_kv,
+    to_peers,
+    from_peers,
+    q_rows,
+    a_rows,
+    fresh,
+    w_sem,
+    kv_sem,
+    cache_sem,
+    send_sem,
+    recv1,
+    recv2,
+    peer_send,
+    peer_recv,
+):
+    lines, across, cores = dims
+    devices = lines * across * cores
+    rows = act_ref.shape[0]
+    chunks = x1.shape[0]
+    width = x1.shape[3]
+    q_cols = wq_ref.shape[1]
+    kv_cols = wkv_ref.shape[1]
+    groups = chunks
+    per_group = HEADS // groups
+    hq = q_cols // HEAD_DIM
+    hkv = kv_cols // HEAD_DIM
+    me = lax.axis_index("mp")
+    core = lax.rem(me, cores)
+    col = lax.rem(me // cores, across)
+    line = me // (cores * across)
+
+    def index(l, a, k):
+        return (l * across + a) * cores + k
+
+    other_lines = [lax.rem(line + i, lines) for i in range(1, lines)]
+    other_cols = [lax.rem(col + i, across) for i in range(1, across)]
+    other_cores = [lax.rem(core + i, cores) for i in range(1, cores)]
+
+    def weights(source, c):
+        return pltpu.make_async_copy(
+            source.at[pl.ds(pl.multiple_of(c * width, width), width), :], wbuf.at[c], w_sem.at[c]
+        )
+
+    kv_copy = pltpu.make_async_copy(wkv_ref, kvbuf, kv_sem.at[0])
+    k_copy = pltpu.make_async_copy(kc_ref, kbuf, cache_sem.at[0])
+    v_copy = pltpu.make_async_copy(vc_ref, vbuf, cache_sem.at[1])
+
+    barrier = pltpu.get_barrier_semaphore()
+
+    @pl.loop(1, devices)
+    def _(i):
+        pl.semaphore_signal(barrier, inc=1, device_id={"mp": lax.rem(me + i, devices)}, device_id_type=MESH)
+
+    kv_copy.start()
+
+    @pl.loop(0, chunks)
+    def _(c):
+        weights(wq_ref, c).start()
+
+    k_copy.start()
+    v_copy.start()
+
+    widened = act_ref[...].astype(jnp.float32)
+    inverse = lax.rsqrt(jnp.mean(widened * widened, axis=-1, keepdims=True) + norm_eps)
+    for c in range(chunks):
+        part = slice(c * width, (c + 1) * width)
+        x1[c, me] = (
+            act_ref[:, part].astype(jnp.float32) * inverse * gain_ref[:, part].astype(jnp.float32)
+        ).astype(jnp.bfloat16)
+
+    pl.semaphore_wait(barrier, devices - 1)
+
+    def copies(x, recv, c):
+        def remote(slot, block, target):
+            return pltpu.make_async_remote_copy(
+                src_ref=x.at[c, block],
+                dst_ref=x.at[c, block],
+                send_sem=send_sem.at[c, slot],
+                recv_sem=recv.at[c, block],
+                device_id={"mp": target},
+                device_id_type=MESH,
+            )
+
+        first, second, third = [], [], []
+        slot = 0
+        for l in other_lines:
+            first.append(remote(slot, me, index(l, col, core)))
+            slot += 1
+        for l in [line] + other_lines:
+            block = index(l, col, core)
+            group = []
+            for a in other_cols:
+                group.append(remote(slot, block, index(line, a, core)))
+                slot += 1
+            for k in other_cores:
+                group.append(remote(slot, block, index(line, col, k)))
+                slot += 1
+            second.append((block, group))
+        for a in other_cols:
+            for l in [line] + other_lines:
+                block = index(l, a, core)
+                group = []
+                for k in other_cores:
+                    group.append(remote(slot, block, index(line, col, k)))
+                    slot += 1
+                third.append((block, group))
+        return first, second, third
+
+    def arrived(x, recv, c, block):
+        pltpu.make_async_remote_copy(
+            src_ref=x.at[c, block],
+            dst_ref=x.at[c, block],
+            send_sem=send_sem.at[c, 0],
+            recv_sem=recv.at[c, block],
+            device_id={"mp": lax.rem(me + 1, devices)},
+            device_id_type=MESH,
+        ).wait_recv()
+
+    def send_own(x, recv, c):
+        first, second, _ = copies(x, recv, c)
+        for copy in first + second[0][1]:
+            copy.start()
+
+    def pass_on(x, recv, c):
+        _, second, _ = copies(x, recv, c)
+        for block, group in second[1:]:
+            arrived(x, recv, c, block)
+            for copy in group:
+                copy.start()
+
+    def finish(x, recv, c):
+        _, _, third = copies(x, recv, c)
+        for block, group in third:
+            arrived(x, recv, c, block)
+            for copy in group:
+                copy.start()
+        for k in other_cores:
+            for a in [col] + other_cols:
+                for l in [line] + other_lines:
+                    arrived(x, recv, c, index(l, a, k))
+
+    def drain(x, recv, c):
+        first, second, third = copies(x, recv, c)
+        for copy in first:
+            copy.wait_send()
+        for _, group in second + third:
+            for copy in group:
+                copy.wait_send()
+
+    def gathered(x, c):
+        block = x[c].astype(jnp.float32).reshape(devices * rows, width)
+        return block.astype(jnp.bfloat16)
+
+    @pl.loop(0, chunks)
+    def _(c):
+        send_own(x1, recv1, c)
+
+    kv_copy.wait()
+    pass_on(x1, recv1, 0)
+    acc[...] = jnp.zeros_like(acc)
+    acc_kv[...] = jnp.zeros_like(acc_kv)
+
+    @pl.loop(0, chunks)
+    def _(c):
+        @pl.when(c + 1 < chunks)
+        def _():
+            pass_on(x1, recv1, c + 1)
+
+        finish(x1, recv1, c)
+        weights(wq_ref, c).wait()
+        x = gathered(x1, c)
+        acc[...] += jnp.dot(x, wbuf[c], preferred_element_type=jnp.float32)
+        acc_kv[...] += jnp.dot(
+            x,
+            kvbuf[pl.ds(pl.multiple_of(c * width, width), width), :],
+            preferred_element_type=jnp.float32,
+        )
+        weights(wo_ref, c).start()
+
+    to_peers[:, :, :q_cols] = acc[...].reshape(devices, rows, q_cols).astype(jnp.bfloat16)
+    to_peers[:, :, q_cols:] = acc_kv[...].reshape(devices, rows, kv_cols).astype(jnp.bfloat16)
+
+    def exchange(i):
+        target = lax.rem(me + i, devices)
+        return pltpu.make_async_remote_copy(
+            src_ref=to_peers.at[target],
+            dst_ref=from_peers.at[me],
+            send_sem=peer_send.at[i],
+            recv_sem=peer_recv.at[me],
+            device_id={"mp": target},
+            device_id_type=MESH,
+        )
+
+    def exchanged(i):
+        source = lax.rem(me + i, devices)
+        return pltpu.make_async_remote_copy(
+            src_ref=to_peers.at[source],
+            dst_ref=from_peers.at[source],
+            send_sem=peer_send.at[i],
+            recv_sem=peer_recv.at[source],
+            device_id={"mp": source},
+            device_id_type=MESH,
+        )
+
+    @pl.loop(1, devices)
+    def _(i):
+        exchange(i).start()
+
+    from_peers[me] = to_peers[me]
+
+    @pl.loop(0, chunks)
+    def _(c):
+        drain(x1, recv1, c)
+
+    k_copy.wait()
+    v_copy.wait()
+
+    @pl.loop(1, devices)
+    def _(i):
+        exchanged(i).wait_recv()
+
+    @pl.loop(1, devices)
+    def _(i):
+        exchange(i).wait_send()
+
+    cosine = cos_ref[...]
+    sine = sin_ref[...]
+    cosine_all = jnp.concatenate([cosine] * per_group, axis=0)
+    sine_all = jnp.concatenate([sine] * per_group, axis=0)
+    scaling = 1.0 / math.sqrt(HEAD_DIM)
+    middle = HEAD_DIM // 2
+
+    def turn(v, c, s):
+        swapped = jnp.concatenate([v[:, middle:], v[:, :middle]], axis=1)
+        return (v * c + swapped * s).astype(jnp.bfloat16).astype(jnp.float32)
+
+    def pair_head(j):
+        if hkv == 1:
+            return from_peers[j, :, q_cols:].astype(jnp.float32)
+        at = pl.multiple_of(q_cols + lax.rem(j, hkv) * HEAD_DIM, HEAD_DIM)
+        return from_peers[j // hkv, :, pl.ds(at, HEAD_DIM)].astype(jnp.float32)
+
+    @pl.loop(0, groups)
+    def _(g):
+        heads = []
+        for h in range(per_group):
+            owner = g * (per_group // hq) + h // hq
+            at = (h % hq) * HEAD_DIM
+            heads.append(from_peers[owner, :, at : at + HEAD_DIM].astype(jnp.float32))
+        q_rows[...] = turn(jnp.concatenate(heads, axis=0), cosine_all, sine_all)
+        fresh[0:rows, :] = turn(pair_head(g), cosine, sine)
+        fresh[rows : 2 * rows, :] = pair_head(groups + g)
+        for r in range(rows):
+            query = q_rows[pl.ds(r, per_group, stride=rows), :]
+            new_key = fresh[r : r + 1, :]
+            new_value = fresh[rows + r : rows + r + 1, :]
+            scores = (
+                lax.dot_general(
+                    query.astype(jnp.bfloat16),
+                    kbuf[r, g],
+                    (((1,), (1,)), ((), ())),
+                    preferred_element_type=jnp.float32,
+                )
+                * scaling
+            )
+            visible = lax.broadcasted_iota(jnp.int32, scores.shape, 1) < len_ref[r]
+            scores = jnp.where(visible, scores, -1e30)
+            own = jnp.sum(query * new_key, axis=-1, keepdims=True) * scaling
+            highest = jnp.maximum(jnp.max(scores, axis=-1, keepdims=True), own)
+            weight = jnp.where(visible, jnp.exp(scores - highest), 0.0)
+            own_weight = jnp.exp(own - highest)
+            denominator = jnp.sum(weight, axis=-1, keepdims=True) + own_weight
+            probs = (weight / denominator).astype(jnp.bfloat16)
+            own_prob = (own_weight / denominator).astype(jnp.bfloat16).astype(jnp.float32)
+            mixed = jnp.dot(probs, vbuf[r, g], preferred_element_type=jnp.float32)
+            a_rows[pl.ds(r, per_group, stride=rows), :] = mixed + own_prob * new_value
+        for h in range(per_group):
+            x2[g, me, :, h * HEAD_DIM : (h + 1) * HEAD_DIM] = a_rows[
+                h * rows : (h + 1) * rows, :
+            ].astype(jnp.bfloat16)
+        send_own(x2, recv2, g)
+
+    pass_on(x2, recv2, 0)
+    acc[...] = jnp.zeros_like(acc)
+
+    @pl.loop(0, chunks)
+    def _(c):
+        @pl.when(c + 1 < chunks)
+        def _():
+            pass_on(x2, recv2, c + 1)
+
+        finish(x2, recv2, c)
+        weights(wo_ref, c).wait()
+        acc[...] += jnp.dot(gathered(x2, c), wbuf[c], preferred_element_type=jnp.float32)
+
+    out_ref[...] = acc[...].astype(jnp.bfloat16)
+
+    @pl.loop(0, chunks)
+    def _(c):
+        drain(x2, recv2, c)
+
+
+def fused_shards(
+    dims, activations, gain, q_weight, kv_weight, o_weight, key_cache, value_cache, lengths
+):
+    devices = dims[0] * dims[1] * dims[2]
+    rows, features = activations.shape
+    q_cols = q_weight.shape[1]
+    kv_cols = kv_weight.shape[1]
+    chunks = KV_HEADS
+    width = features // chunks
+    middle = HEAD_DIM // 2
+    offsets = jnp.arange(middle, dtype=jnp.float32)
+    frequency = jnp.exp(offsets * (-2.0 * math.log(rope_base) / HEAD_DIM))
+    angles = lengths.astype(jnp.float32)[:, None] * frequency
+    cosine = jnp.cos(angles)
+    sine = jnp.sin(angles)
+    sends = devices - 1
+    vmem = pl.BlockSpec(memory_space=pltpu.VMEM)
+    hbm = pl.BlockSpec(memory_space=pl.ANY)
+    dma = pltpu.SemaphoreType.DMA
+    return pl.pallas_call(
+        functools.partial(fused, dims),
+        out_shape=jax.ShapeDtypeStruct((devices * rows, o_weight.shape[1]), jnp.bfloat16),
+        in_specs=[vmem] * 4 + [pl.BlockSpec(memory_space=pltpu.SMEM)] + [hbm] * 5,
+        out_specs=vmem,
+        scratch_shapes=[
+            pltpu.VMEM((chunks, width, q_cols), jnp.bfloat16),
+            pltpu.VMEM(kv_weight.shape, jnp.bfloat16),
+            pltpu.VMEM(key_cache.shape, jnp.bfloat16),
+            pltpu.VMEM(value_cache.shape, jnp.bfloat16),
+            pltpu.VMEM((chunks, devices, rows, width), jnp.bfloat16),
+            pltpu.VMEM((chunks, devices, rows, width), jnp.bfloat16),
+            pltpu.VMEM((devices * rows, q_cols), jnp.float32),
+            pltpu.VMEM((devices * rows, kv_cols), jnp.float32),
+            pltpu.VMEM((devices, rows, q_cols + kv_cols), jnp.bfloat16),
+            pltpu.VMEM((devices, rows, q_cols + kv_cols), jnp.bfloat16),
+            pltpu.VMEM((HEADS // KV_HEADS * rows, HEAD_DIM), jnp.float32),
+            pltpu.VMEM((HEADS // KV_HEADS * rows, HEAD_DIM), jnp.float32),
+            pltpu.VMEM((2 * rows, HEAD_DIM), jnp.float32),
+            dma((chunks,)),
+            dma((1,)),
+            dma((2,)),
+            dma((chunks, sends)),
+            dma((chunks, devices)),
+            dma((chunks, devices)),
+            dma((devices,)),
+            dma((devices,)),
+        ],
+        compiler_params=pltpu.CompilerParams(
+            collective_id=0, has_side_effects=True, vmem_limit_bytes=62 * 1024 * 1024
+        ),
+    )(
+        activations,
+        gain.reshape(1, features),
+        jnp.concatenate([cosine, cosine], axis=1),
+        jnp.concatenate([-sine, sine], axis=1),
+        lengths,
+        q_weight,
+        kv_weight,
+        o_weight,
+        key_cache,
+        value_cache,
+    )
+
+
+def fits(mesh):
+    devices = mesh.shape["mp"]
+    per_group = HEADS // KV_HEADS
+    heads = HEADS // devices if HEADS % devices == 0 else 0
+    pairs = 2 * KV_HEADS // devices if 2 * KV_HEADS % devices == 0 else 0
+    return heads > 0 and pairs > 0 and per_group % heads == 0
+
 
 def solution(mesh):
     placed = (
@@ -105,6 +520,7 @@
         P(("groups", "mp"), None, None, None),
         P(("groups", "mp")),
     )
+    body = functools.partial(fused_shards, layout_of(mesh)) if fits(mesh) else shards
     return jax.shard_map(
-        shards, mesh=mesh, in_specs=placed, out_specs=P("groups", "mp"), check_vma=False
-    )
+        body, mesh=mesh, in_specs=placed, out_specs=P("groups", "mp"), check_vma=False
+    )

time: 162 us -> 79.8 us (0.49)
  waiting for transfers between devices: 89.9 us -> 0 us
  Pallas kernels: 0 us -> 75.2 us
  matrix products: 36.2 us -> 0 us
  between operations: 13.5 us -> 0.02 us
  starting transfers between devices: 9.48 us -> 0 us
  other arithmetic: 5.85 us -> 1.44 us
  local copies, waits for them, and re-layouts: 6.73 us -> 2.99 us
    all_gather x2 -> x0, waiting for transfers between devices: 82.2 us -> none  [the longest x1 42.8 us: shards(): piece = lax.all_gather(normed, 'mp', axis=0, tiled=True)]
    pallas_call x0 -> x1, Pallas kernels: none -> 75.2 us  [fused_shards(): pl.pallas_call(functools.partial(fused, dims), out_shape=jax.ShapeDtypeSt...]
    dot_general x6 -> x0, matrix products: 36.2 us -> none  [the longest x1 14.2 us: shards(): jnp.dot(lax.all_gather(attended, 'mp', axis=0, tiled=True), o_weight, pre...]
    all_to_all x2 -> x0, starting transfers between devices: 9.44 us -> none  [the longest x1 5.97 us: shards(): lax.all_to_all(projected[:, :query_cols], 'mp', split_axis=0, concat_axis...]
    all_to_all x2 -> x0, waiting for transfers between devices: 7.67 us -> none  [the longest x1 7.67 us: shards(): lax.all_to_all(projected[:, :query_cols], 'mp', split_axis=0, concat_axis...]
    unnamed x5 -> x1, local copies, waits for them, and re-layouts: 5.81 us -> 1.57 us
    unnamed x2 -> x0, other arithmetic: 1.71 us -> none
  transfers between devices with their start and end apart: 4 -> 0, of which waited for: 3 -> 0; matrix products, arithmetic and copies ran while one was open for 9% -> 0% of each run, Pallas kernels for 0% -> 0%
where the time goes in v1:
time: 79.8 us; the launch traced here: 79.6 us
  Pallas kernels  75.2 us (94%)
  local copies, waits for them, and re-layouts  2.99 us (4%)
  other arithmetic  1.44 us (2%)
    pallas_call x1, Pallas kernels, fused_shards(): pl.pallas_call(functools.partial(fused, dims), out_shape=jax.ShapeDtypeSt...  75.2 us

profile of v1, /device:TPU:0, one launch (start us, length us, event | category | flops | bytes accessed | tf_op | source)
XLA Modules:
  0.0 79.6 jit_solution(5988695409891844744)
XLA Ops:
  0.0 0.7 convert_element_type.3
  0.7 0.1 fusion
  0.8 0.7 pad_maximum_fusion
  1.4 1.4 %reshape.9.gain_ref = bf16[1,16384]{1,0:T(2,128)(2,1)} reshape(bf16[16384]{0:T(1024)(128)(2,1)} %param.9) | data formatting | bytes 65536 | tf_op jit(solution)/shard_map/reshape | solution.py:492
  2.9 75.2 %shard_map.82 = bf16[64,1024]{1,0:T(8,128)(2,1)} custom-call(bf16[4,16384]{1,0:T(4,128)(2,1)} %act_ref.1, bf16[1,16384]{1,0:T(2,128)(2,1)} %reshape.9.gain_ref, f32[4,128]{1,0:T(4,128)} %get-tuple-element.8.cos_ref, f32[4,128]{1,0:T(4,128)} %get-tuple-element.9.sin_ref, s32[4]{0:T(128)} %len_ref.1, bf16[16384,1024]{1,0:T(8,128)(2,1)} %wq_ref.1, ...), custom_call_target="tpu_custom_call" | custom-call | tf_op jit(solution)/shard_map/pallas_call | solution.py:459
  78.1 1.6 %copy.10 = bf16[64,1024]{1,0:T(8,128)(2,1)} copy(bf16[64,1024]{1,0:T(8,128)(2,1)} %shard_map.82) | data formatting | bytes 262144
  (1 shorter events, 0.0 us)

commit v2 on v1

--- a/solution.py
+++ b/solution.py
@@ -119,8 +119,6 @@
     dims,
     act_ref,
     gain_ref,
-    cos_ref,
-    sin_ref,
     len_ref,
     wq_ref,
     wkv_ref,
@@ -141,6 +139,7 @@
     q_rows,
     a_rows,
     fresh,
+    tables,
     w_sem,
     kv_sem,
     cache_sem,
@@ -202,7 +201,7 @@
     for c in range(chunks):
         part = slice(c * width, (c + 1) * width)
         x1[c, me] = (
-            act_ref[:, part].astype(jnp.float32) * inverse * gain_ref[:, part].astype(jnp.float32)
+            act_ref[:, part].astype(jnp.float32) * inverse * gain_ref[part].astype(jnp.float32)
         ).astype(jnp.bfloat16)
 
     pl.semaphore_wait(barrier, devices - 1)
@@ -271,6 +270,8 @@
             arrived(x, recv, c, block)
             for copy in group:
                 copy.start()
+
+    def settle(x, recv, c):
         for k in other_cores:
             for a in [col] + other_cols:
                 for l in [line] + other_lines:
@@ -292,18 +293,37 @@
     def _(c):
         send_own(x1, recv1, c)
 
+    middle = HEAD_DIM // 2
+    lane = lax.broadcasted_iota(jnp.int32, (rows, HEAD_DIM), 1)
+    which = lax.broadcasted_iota(jnp.int32, (rows, HEAD_DIM), 0)
+    position = jnp.zeros((rows, HEAD_DIM), jnp.float32)
+    for r in range(rows):
+        position = jnp.where(which == r, len_ref[r].astype(jnp.float32), position)
+    offsets = jnp.where(lane < middle, lane, lane - middle).astype(jnp.float32)
+    angles = position * jnp.exp(offsets * (-2.0 * math.log(rope_base) / HEAD_DIM))
+    sine = jnp.sin(angles)
+    tables[0] = jnp.concatenate([jnp.cos(angles)] * per_group, axis=0)
+    tables[1] = jnp.concatenate([jnp.where(lane < middle, -sine, sine)] * per_group, axis=0)
+
     kv_copy.wait()
-    pass_on(x1, recv1, 0)
     acc[...] = jnp.zeros_like(acc)
     acc_kv[...] = jnp.zeros_like(acc_kv)
+    early = min(2, chunks)
+    for c in range(early):
+        pass_on(x1, recv1, c)
+    finish(x1, recv1, 0)
 
     @pl.loop(0, chunks)
     def _(c):
+        @pl.when(c + early < chunks)
+        def _():
+            pass_on(x1, recv1, c + early)
+
         @pl.when(c + 1 < chunks)
         def _():
-            pass_on(x1, recv1, c + 1)
-
-        finish(x1, recv1, c)
+            finish(x1, recv1, c + 1)
+
+        settle(x1, recv1, c)
         weights(wq_ref, c).wait()
         x = gathered(x1, c)
         acc[...] += jnp.dot(x, wbuf[c], preferred_element_type=jnp.float32)
@@ -360,12 +380,7 @@
     def _(i):
         exchange(i).wait_send()
 
-    cosine = cos_ref[...]
-    sine = sin_ref[...]
-    cosine_all = jnp.concatenate([cosine] * per_group, axis=0)
-    sine_all = jnp.concatenate([sine] * per_group, axis=0)
     scaling = 1.0 / math.sqrt(HEAD_DIM)
-    middle = HEAD_DIM // 2
 
     def turn(v, c, s):
         swapped = jnp.concatenate([v[:, middle:], v[:, :middle]], axis=1)
@@ -377,56 +392,76 @@
         at = pl.multiple_of(q_cols + lax.rem(j, hkv) * HEAD_DIM, HEAD_DIM)
         return from_peers[j // hkv, :, pl.ds(at, HEAD_DIM)].astype(jnp.float32)
 
+    passing = min(3, chunks)
+    finishing = min(5, chunks)
+
     @pl.loop(0, groups)
     def _(g):
+        @pl.when(g >= passing)
+        def _():
+            pass_on(x2, recv2, g - passing)
+
+        @pl.when(g >= finishing)
+        def _():
+            finish(x2, recv2, g - finishing)
+
         heads = []
         for h in range(per_group):
             owner = g * (per_group // hq) + h // hq
             at = (h % hq) * HEAD_DIM
             heads.append(from_peers[owner, :, at : at + HEAD_DIM].astype(jnp.float32))
-        q_rows[...] = turn(jnp.concatenate(heads, axis=0), cosine_all, sine_all)
-        fresh[0:rows, :] = turn(pair_head(g), cosine, sine)
+        q_rows[...] = turn(jnp.concatenate(heads, axis=0), tables[0], tables[1])
+        fresh[0:rows, :] = turn(pair_head(g), tables[0, 0:rows, :], tables[1, 0:rows, :])
         fresh[rows : 2 * rows, :] = pair_head(groups + g)
+        slots = kbuf.shape[2]
+        slot = lax.broadcasted_iota(jnp.int32, (per_group, slots), 1)
+        scores, own = [], []
         for r in range(rows):
             query = q_rows[pl.ds(r, per_group, stride=rows), :]
-            new_key = fresh[r : r + 1, :]
-            new_value = fresh[rows + r : rows + r + 1, :]
-            scores = (
-                lax.dot_general(
-                    query.astype(jnp.bfloat16),
-                    kbuf[r, g],
-                    (((1,), (1,)), ((), ())),
-                    preferred_element_type=jnp.float32,
-                )
-                * scaling
+            own.append(jnp.sum(query * fresh[r : r + 1, :], axis=-1, keepdims=True))
+            part = lax.dot_general(
+                query.astype(jnp.bfloat16),
+                kbuf[r, g],
+                (((1,), (1,)), ((), ())),
+                preferred_element_type=jnp.float32,
             )
-            visible = lax.broadcasted_iota(jnp.int32, scores.shape, 1) < len_ref[r]
-            scores = jnp.where(visible, scores, -1e30)
-            own = jnp.sum(query * new_key, axis=-1, keepdims=True) * scaling
-            highest = jnp.maximum(jnp.max(scores, axis=-1, keepdims=True), own)
-            weight = jnp.where(visible, jnp.exp(scores - highest), 0.0)
-            own_weight = jnp.exp(own - highest)
-            denominator = jnp.sum(weight, axis=-1, keepdims=True) + own_weight
-            probs = (weight / denominator).astype(jnp.bfloat16)
-            own_prob = (own_weight / denominator).astype(jnp.bfloat16).astype(jnp.float32)
-            mixed = jnp.dot(probs, vbuf[r, g], preferred_element_type=jnp.float32)
-            a_rows[pl.ds(r, per_group, stride=rows), :] = mixed + own_prob * new_value
+            scores.append(jnp.where(slot < len_ref[r], part * scaling, -1e30))
+        scores = jnp.concatenate(scores, axis=0)
+        own = jnp.concatenate(own, axis=0) * scaling
+        highest = jnp.maximum(jnp.max(scores, axis=-1, keepdims=True), own)
+        weight = jnp.exp(scores - highest)
+        own_weight = jnp.exp(own - highest)
+        scale = 1.0 / (jnp.sum(weight, axis=-1, keepdims=True) + own_weight)
+        probs = (weight * scale).astype(jnp.bfloat16)
+        own_prob = (own_weight * scale).astype(jnp.bfloat16).astype(jnp.float32)
+        mixed = []
+        for r in range(rows):
+            at = slice(r * per_group, (r + 1) * per_group)
+            mixed.append(
+                jnp.dot(probs[at], vbuf[r, g], preferred_element_type=jnp.float32)
+                + own_prob[at] * fresh[rows + r : rows + r + 1, :]
+            )
+        for r in range(rows):
+            a_rows[pl.ds(r, per_group, stride=rows), :] = mixed[r]
         for h in range(per_group):
             x2[g, me, :, h * HEAD_DIM : (h + 1) * HEAD_DIM] = a_rows[
                 h * rows : (h + 1) * rows, :
             ].astype(jnp.bfloat16)
         send_own(x2, recv2, g)
 
-    pass_on(x2, recv2, 0)
     acc[...] = jnp.zeros_like(acc)
 
     @pl.loop(0, chunks)
     def _(c):
-        @pl.when(c + 1 < chunks)
+        @pl.when(c + chunks - passing < chunks)
         def _():
-            pass_on(x2, recv2, c + 1)
-
-        finish(x2, recv2, c)
+            pass_on(x2, recv2, c + chunks - passing)
+
+        @pl.when(c + chunks - finishing < chunks)
+        def _():
+            finish(x2, recv2, c + chunks - finishing)
+
+        settle(x2, recv2, c)
         weights(wo_ref, c).wait()
         acc[...] += jnp.dot(gathered(x2, c), wbuf[c], preferred_element_type=jnp.float32)
 
@@ -446,12 +481,6 @@
     kv_cols = kv_weight.shape[1]
     chunks = KV_HEADS
     width = features // chunks
-    middle = HEAD_DIM // 2
-    offsets = jnp.arange(middle, dtype=jnp.float32)
-    frequency = jnp.exp(offsets * (-2.0 * math.log(rope_base) / HEAD_DIM))
-    angles = lengths.astype(jnp.float32)[:, None] * frequency
-    cosine = jnp.cos(angles)
-    sine = jnp.sin(angles)
     sends = devices - 1
     vmem = pl.BlockSpec(memory_space=pltpu.VMEM)
     hbm = pl.BlockSpec(memory_space=pl.ANY)
@@ -459,7 +488,7 @@
     return pl.pallas_call(
         functools.partial(fused, dims),
         out_shape=jax.ShapeDtypeStruct((devices * rows, o_weight.shape[1]), jnp.bfloat16),
-        in_specs=[vmem] * 4 + [pl.BlockSpec(memory_space=pltpu.SMEM)] + [hbm] * 5,
+        in_specs=[vmem] * 2 + [pl.BlockSpec(memory_space=pltpu.SMEM)] + [hbm] * 5,
         out_specs=vmem,
         scratch_shapes=[
             pltpu.VMEM((chunks, width, q_cols), jnp.bfloat16),
@@ -475,6 +504,7 @@
             pltpu.VMEM((HEADS // KV_HEADS * rows, HEAD_DIM), jnp.float32),
             pltpu.VMEM((HEADS // KV_HEADS * rows, HEAD_DIM), jnp.float32),
             pltpu.VMEM((2 * rows, HEAD_DIM), jnp.float32),
+            pltpu.VMEM((2, HEADS // KV_HEADS * rows, HEAD_DIM), jnp.float32),
             dma((chunks,)),
             dma((1,)),
             dma((2,)),
@@ -489,9 +519,7 @@
         ),
     )(
         activations,
-        gain.reshape(1, features),
-        jnp.concatenate([cosine, cosine], axis=1),
-        jnp.concatenate([-sine, sine], axis=1),
+        gain,
         lengths,
         q_weight,
         kv_weight,

time: 79.8 us -> 64.5 us (0.81)
  Pallas kernels: 75.2 us -> 62.8 us
  other arithmetic: 1.44 us -> 0 us
  local copies, waits for them, and re-layouts: 2.99 us -> 1.57 us
    pallas_call x1, Pallas kernels: 75.2 us -> 62.8 us  [fused_shards(): pl.pallas_call(functools.partial(fused, dims), out_shape=jax.ShapeDtypeSt...]
    reshape x1 -> x0, local copies, waits for them, and re-layouts: 1.42 us -> none  [fused_shards(): gain.reshape(1, features)]
where the time goes in v2:
time: 64.5 us; the launch traced here: 64.3 us
  Pallas kernels  62.8 us (97%)
  local copies, waits for them, and re-layouts  1.57 us (2%)
    pallas_call x1, Pallas kernels, fused_shards(): pl.pallas_call(functools.partial(fused, dims), out_shape=jax.ShapeDtypeSt...  62.8 us
    unnamed x1, local copies, waits for them, and re-layouts  1.57 us

profile of v2, /device:TPU:0, one launch (start us, length us, event | category | flops | bytes accessed | tf_op | source)
XLA Modules:
  0.0 64.3 jit_solution(15822204006721240620)
XLA Ops:
  0.0 62.8 %shard_map.82 = bf16[64,1024]{1,0:T(8,128)(2,1)} custom-call(bf16[4,16384]{1,0:T(4,128)(2,1)} %act_ref.1, bf16[16384]{0:T(1024)(128)(2,1)} %gain_ref.1, s32[4]{0:T(128)} %len_ref.1, bf16[16384,1024]{1,0:T(8,128)(2,1)} %wq_ref.1, bf16[16384,128]{1,0:T(8,128)(2,1)} %wkv_ref.1, bf16[16384,1024]{1,0:T(8,128)(2,1)} %wo_ref.1, bf16[4,8,512,128]{3,2,1,0:T(8,128)(2,1)} %kc_ref.1, ...), custom_call_target="tpu_custom_call" | custom-call | tf_op jit(solution)/shard_map/pallas_call | solution.py:488
  62.8 1.6 %copy.10 = bf16[64,1024]{1,0:T(8,128)(2,1)} copy(bf16[64,1024]{1,0:T(8,128)(2,1)} %shard_map.82) | data formatting | bytes 262144

commit v3 on v2

--- a/solution.py
+++ b/solution.py
@@ -168,6 +168,14 @@
     def index(l, a, k):
         return (l * across + a) * cores + k
 
+    def place(l, a, k):
+        return (k * across + a) * lines + l
+
+    def place_of(device):
+        rest = device // cores
+        return place(rest // across, lax.rem(rest, across), lax.rem(device, cores))
+
+    mine = place(line, col, core)
     other_lines = [lax.rem(line + i, lines) for i in range(1, lines)]
     other_cols = [lax.rem(col + i, across) for i in range(1, across)]
     other_cores = [lax.rem(core + i, cores) for i in range(1, cores)]
@@ -200,90 +208,73 @@
     inverse = lax.rsqrt(jnp.mean(widened * widened, axis=-1, keepdims=True) + norm_eps)
     for c in range(chunks):
         part = slice(c * width, (c + 1) * width)
-        x1[c, me] = (
+        x1[c, mine] = (
             act_ref[:, part].astype(jnp.float32) * inverse * gain_ref[part].astype(jnp.float32)
         ).astype(jnp.bfloat16)
 
     pl.semaphore_wait(barrier, devices - 1)
 
-    def copies(x, recv, c):
-        def remote(slot, block, target):
-            return pltpu.make_async_remote_copy(
-                src_ref=x.at[c, block],
-                dst_ref=x.at[c, block],
-                send_sem=send_sem.at[c, slot],
-                recv_sem=recv.at[c, block],
-                device_id={"mp": target},
-                device_id_type=MESH,
+    def remote(x, recv, c, at, size, slot, arrival, target):
+        return pltpu.make_async_remote_copy(
+            src_ref=x.at[c, pl.ds(at, size)],
+            dst_ref=x.at[c, pl.ds(at, size)],
+            send_sem=send_sem.at[c, slot],
+            recv_sem=recv.at[c, arrival],
+            device_id={"mp": target},
+            device_id_type=MESH,
+        )
+
+    def to_lines(x, recv, c):
+        return [
+            remote(x, recv, c, mine, 1, i, line, index(l, col, core))
+            for i, l in enumerate(other_lines)
+        ]
+
+    def to_cols(x, recv, c):
+        at = place(0, col, core)
+        return [
+            remote(x, recv, c, at, lines, lines + i, lines + col, index(line, a, core))
+            for i, a in enumerate(other_cols)
+        ]
+
+    def to_cores(x, recv, c):
+        at = place(0, 0, core)
+        return [
+            remote(
+                x, recv, c, at, lines * across, lines + across + i,
+                lines + across + core, index(line, col, k),
             )
-
-        first, second, third = [], [], []
-        slot = 0
+            for i, k in enumerate(other_cores)
+        ]
+
+    def send_own(x, recv, c):
+        for copy in to_lines(x, recv, c):
+            copy.start()
+
+    def pass_on(x, recv, c):
         for l in other_lines:
-            first.append(remote(slot, me, index(l, col, core)))
-            slot += 1
-        for l in [line] + other_lines:
-            block = index(l, col, core)
-            group = []
-            for a in other_cols:
-                group.append(remote(slot, block, index(line, a, core)))
-                slot += 1
-            for k in other_cores:
-                group.append(remote(slot, block, index(line, col, k)))
-                slot += 1
-            second.append((block, group))
+            remote(x, recv, c, place(l, col, core), 1, 0, l, index(l, col, core)).wait_recv()
+        for copy in to_cols(x, recv, c):
+            copy.start()
+
+    def finish(x, recv, c):
         for a in other_cols:
-            for l in [line] + other_lines:
-                block = index(l, a, core)
-                group = []
-                for k in other_cores:
-                    group.append(remote(slot, block, index(line, col, k)))
-                    slot += 1
-                third.append((block, group))
-        return first, second, third
-
-    def arrived(x, recv, c, block):
-        pltpu.make_async_remote_copy(
-            src_ref=x.at[c, block],
-            dst_ref=x.at[c, block],
-            send_sem=send_sem.at[c, 0],
-            recv_sem=recv.at[c, block],
-            device_id={"mp": lax.rem(me + 1, devices)},
-            device_id_type=MESH,
-        ).wait_recv()
-
-    def send_own(x, recv, c):
-        first, second, _ = copies(x, recv, c)
-        for copy in first + second[0][1]:
+            remote(
+                x, recv, c, place(0, a, core), lines, 0, lines + a, index(line, a, core)
+            ).wait_recv()
+        for copy in to_cores(x, recv, c):
             copy.start()
-
-    def pass_on(x, recv, c):
-        _, second, _ = copies(x, recv, c)
-        for block, group in second[1:]:
-            arrived(x, recv, c, block)
-            for copy in group:
-                copy.start()
-
-    def finish(x, recv, c):
-        _, _, third = copies(x, recv, c)
-        for block, group in third:
-            arrived(x, recv, c, block)
-            for copy in group:
-                copy.start()
 
     def settle(x, recv, c):
         for k in other_cores:
-            for a in [col] + other_cols:
-                for l in [line] + other_lines:
-                    arrived(x, recv, c, index(l, a, k))
+            remote(
+                x, recv, c, place(0, 0, k), lines * across, 0, lines + across + k,
+                index(line, col, k),
+            ).wait_recv()
 
     def drain(x, recv, c):
-        first, second, third = copies(x, recv, c)
-        for copy in first:
+        for copy in to_lines(x, recv, c) + to_cols(x, recv, c) + to_cores(x, recv, c):
             copy.wait_send()
-        for _, group in second + third:
-            for copy in group:
-                copy.wait_send()
 
     def gathered(x, c):
         block = x[c].astype(jnp.float32).reshape(devices * rows, width)
@@ -340,7 +331,7 @@
     def exchange(i):
         target = lax.rem(me + i, devices)
         return pltpu.make_async_remote_copy(
-            src_ref=to_peers.at[target],
+            src_ref=to_peers.at[place_of(target)],
             dst_ref=from_peers.at[me],
             send_sem=peer_send.at[i],
             recv_sem=peer_recv.at[me],
@@ -351,7 +342,7 @@
     def exchanged(i):
         source = lax.rem(me + i, devices)
         return pltpu.make_async_remote_copy(
-            src_ref=to_peers.at[source],
+            src_ref=to_peers.at[place_of(source)],
             dst_ref=from_peers.at[source],
             send_sem=peer_send.at[i],
             recv_sem=peer_recv.at[source],
@@ -363,7 +354,7 @@
     def _(i):
         exchange(i).start()
 
-    from_peers[me] = to_peers[me]
+    from_peers[me] = to_peers[mine]
 
     @pl.loop(0, chunks)
     def _(c):
@@ -444,7 +435,7 @@
         for r in range(rows):
             a_rows[pl.ds(r, per_group, stride=rows), :] = mixed[r]
         for h in range(per_group):
-            x2[g, me, :, h * HEAD_DIM : (h + 1) * HEAD_DIM] = a_rows[
+            x2[g, mine, :, h * HEAD_DIM : (h + 1) * HEAD_DIM] = a_rows[
                 h * rows : (h + 1) * rows, :
             ].astype(jnp.bfloat16)
         send_own(x2, recv2, g)
@@ -465,7 +456,12 @@
         weights(wo_ref, c).wait()
         acc[...] += jnp.dot(gathered(x2, c), wbuf[c], preferred_element_type=jnp.float32)
 
-    out_ref[...] = acc[...].astype(jnp.bfloat16)
+    ordered = []
+    for l in range(lines):
+        for a in range(across):
+            for k in range(cores):
+                ordered.append(acc[place(l, a, k) * rows : (place(l, a, k) + 1) * rows, :])
+    out_ref[...] = jnp.concatenate(ordered, axis=0).astype(jnp.bfloat16)
 
     @pl.loop(0, chunks)
     def _(c):
@@ -481,7 +477,7 @@
     kv_cols = kv_weight.shape[1]
     chunks = KV_HEADS
     width = features // chunks
-    sends = devices - 1
+    sends = sum(dims)
     vmem = pl.BlockSpec(memory_space=pltpu.VMEM)
     hbm = pl.BlockSpec(memory_space=pl.ANY)
     dma = pltpu.SemaphoreType.DMA
@@ -509,8 +505,8 @@
             dma((1,)),
             dma((2,)),
             dma((chunks, sends)),
-            dma((chunks, devices)),
-            dma((chunks, devices)),
+            dma((chunks, sends)),
+            dma((chunks, sends)),
             dma((devices,)),
             dma((devices,)),
         ],

time: 64.5 us -> 64 us (level)
  no operation moved by 1% of the time
where the time goes in v3:
time: 64 us; the launch traced here: 63.9 us
  Pallas kernels  62.3 us (97%)
  local copies, waits for them, and re-layouts  1.57 us (2%)
    pallas_call x1, Pallas kernels, fused_shards(): pl.pallas_call(functools.partial(fused, dims), out_shape=jax.ShapeDtypeSt...  62.3 us
    unnamed x1, local copies, waits for them, and re-layouts  1.57 us

profile of v3, /device:TPU:0, one launch (start us, length us, event | category | flops | bytes accessed | tf_op | source)
XLA Modules:
  0.0 63.9 jit_solution(2472861174674615444)
XLA Ops:
  0.0 62.3 %shard_map.82 = bf16[64,1024]{1,0:T(8,128)(2,1)} custom-call(bf16[4,16384]{1,0:T(4,128)(2,1)} %act_ref.1, bf16[16384]{0:T(1024)(128)(2,1)} %gain_ref.1, s32[4]{0:T(128)} %len_ref.1, bf16[16384,1024]{1,0:T(8,128)(2,1)} %wq_ref.1, bf16[16384,128]{1,0:T(8,128)(2,1)} %wkv_ref.1, bf16[16384,1024]{1,0:T(8,128)(2,1)} %wo_ref.1, bf16[4,8,512,128]{3,2,1,0:T(8,128)(2,1)} %kc_ref.1, ...), custom_call_target="tpu_custom_call" | custom-call | tf_op jit(solution)/shard_map/pallas_call | solution.py:484
  62.3 1.6 %copy.10 = bf16[64,1024]{1,0:T(8,128)(2,1)} copy(bf16[64,1024]{1,0:T(8,128)(2,1)} %shard_map.82) | data formatting | bytes 262144
